TPU v7x, 32 devices: a whole 2x2x4 slice. The times are simulated.
32 devices in a mesh: dp: 16 (over z, y, x), tensor: 2 (over core).
Axes of the slice: x: 2, y: 2, z: 4, core: 2. Of those that a mesh axis runs over, the one named last changes fastest.
Arguments:
- tokens: bfloat16 [16, 2048, 512], P('dp', 'tensor'), may hold values from -6 to 6
- cotangent: bfloat16 [16, 2048, 512], P('dp', 'tensor'), may hold values from -6 to 6
- span_ids: int32 [16, 8, 256], P('dp'), may hold values from 0 to 1, never falling along the last dimension, each value on 1 to 192 neighbouring positions
- gain_one: float32 [512], replicated, may hold values from 0.25 to 1.75
- w_qkv: bfloat16 [512, 3, 512], P('dp', None, 'tensor'), may hold values from -0.25 to 0.25
- w_out: bfloat16 [512, 512], P('tensor', 'dp'), may hold values from -1 to 1
- b_out: float32 [512], replicated, may hold values from -3 to 3
- gain_two: float32 [512], replicated, may hold values from 0.25 to 1.75
- w_up: bfloat16 [512, 2048], P('dp', 'tensor'), may hold values from -0.25 to 0.25
- b_up: float32 [2048], P('tensor'), may hold values from -3 to 3
- w_down: bfloat16 [2048, 512], P('tensor', 'dp'), may hold values from -0.125 to 0.125
- b_down: float32 [512], replicated, may hold values from -3 to 3
Outputs:
- result: bfloat16 [16, 2048, 512], P('dp', 'tensor')
- d_tokens: bfloat16 [16, 2048, 512], P('dp', 'tensor')
- d_gain_one: float32 [512], replicated
- d_w_qkv: float32 [512, 3, 512], P('dp', None, 'tensor')
- d_w_out: float32 [512, 512], P('tensor', 'dp')
- d_b_out: float32 [512], replicated
- d_gain_two: float32 [512], replicated
- d_w_up: float32 [512, 2048], P('dp', 'tensor')
- d_b_up: float32 [2048], replicated
- d_w_down: float32 [2048, 512], P('tensor', 'dp')
- d_b_down: float32 [512], replicated
Inputs may be any that keep to these rules, and one draw needn't show every extreme that they name: `span_ids`: within each block of 256 positions the span numbers never fall and each of the 2 spans holds 1 to 192 positions.
All inputs are finite; a program needn't handle non-finite values.
Results may differ from a plain program's by a relative error of at most 0.014.
Values may be sent and summed in bfloat16 or wider, within the bound.
A program may use at most 128 MiB of HBM per device.

v0:
```python
import math
import jax
import jax.numpy as jnp
from jax import lax
from jax.sharding import PartitionSpec as P

HD = 64
BLK = 256
SPB = 2
epsilon = 1e-05
masked = -1e30


def normalize(values, gain_vec):
    centre = values - jnp.mean(values, axis=-1, keepdims=True)
    spread = jnp.mean(centre * centre, axis=-1, keepdims=True)
    inverse = lax.rsqrt(spread + epsilon)
    unit_rows = centre * inverse
    return (unit_rows, inverse, unit_rows * gain_vec)


def normalize_back(incoming_grad, unit_rows, inverse, gain_vec):
    scaled = incoming_grad * gain_vec
    mean_one = jnp.mean(scaled, axis=-1, keepdims=True)
    mean_two = jnp.mean(scaled * unit_rows, axis=-1, keepdims=True)
    return (
        inverse * (scaled - mean_one - unit_rows * mean_two),
        jnp.sum(incoming_grad * unit_rows, axis=0),
    )


def pair_rows(values):
    return lax.all_gather(values, "tensor", axis=0, tiled=True)


def pair_sums(term_fn, rows):
    return lax.psum_scatter(
        term_fn(jnp.int32(0), rows * lax.axis_size("tensor")).astype(jnp.bfloat16),
        "tensor",
        scatter_dimension=0,
        tiled=True,
    ).astype(jnp.float32)


def scores(queries, key_rows, key_sum, counts_all, allowed):
    scaling = 1.0 / math.sqrt(queries.shape[-1])
    near_scores = (
        jnp.einsum("bie,bje->bij", queries, key_rows, preferred_element_type=jnp.float32) * scaling
    )
    far_scores = (
        jnp.einsum("bie,ce->bic", queries, key_sum, preferred_element_type=jnp.float32) * scaling
    )
    far_scores = far_scores + jnp.log(counts_all).reshape(-1)
    far_scores = jnp.where(allowed[:, None, :], far_scores, masked)
    return (near_scores, far_scores)


def span_means(key_rows, value_rows, member_low, counts):
    head_size = key_rows.shape[-1]
    key_sum = jnp.einsum("bjm,bje->bme", member_low, key_rows, preferred_element_type=jnp.float32)
    value_sum = jnp.einsum(
        "bjm,bje->bme", member_low, value_rows, preferred_element_type=jnp.float32
    )
    key_sum = (key_sum / counts[:, :, None]).astype(jnp.bfloat16).reshape(-1, head_size)
    value_sum = (value_sum / counts[:, :, None]).astype(jnp.bfloat16).reshape(-1, head_size)
    return (key_sum, value_sum)


def attend(queries, key_rows, value_rows, key_sum, value_sum, counts_all, allowed):
    near_scores, far_scores = scores(queries, key_rows, key_sum, counts_all, allowed)
    largest = jnp.maximum(jnp.max(near_scores, axis=-1), jnp.max(far_scores, axis=-1))
    near_exp = jnp.exp(near_scores - largest[..., None])
    far_exp = jnp.exp(far_scores - largest[..., None])
    denominator = jnp.sum(near_exp, axis=-1) + jnp.sum(far_exp, axis=-1)
    near_prob = (near_exp / denominator[..., None]).astype(jnp.bfloat16)
    far_prob = (far_exp / denominator[..., None]).astype(jnp.bfloat16)
    attended = jnp.einsum("bij,bje->bie", near_prob, value_rows, preferred_element_type=jnp.float32)
    attended = attended + jnp.einsum(
        "bic,ce->bie", far_prob, value_sum, preferred_element_type=jnp.float32
    )
    return (attended.astype(jnp.bfloat16), largest + jnp.log(denominator))


def head_backward(
    queries, key_rows, value_rows, grad_heads, log_total, key_sum, value_sum, counts_all, allowed
):
    scaling = 1.0 / math.sqrt(queries.shape[-1])
    near_scores, far_scores = scores(queries, key_rows, key_sum, counts_all, allowed)
    near_prob = jnp.exp(near_scores - log_total[..., None])
    far_prob = jnp.exp(far_scores - log_total[..., None])
    grad_value = jnp.einsum(
        "bij,bie->bje",
        near_prob.astype(jnp.bfloat16),
        grad_heads,
        preferred_element_type=jnp.float32,
    )
    grad_vsum = jnp.einsum(
        "bic,bie->ce", far_prob.astype(jnp.bfloat16), grad_heads, preferred_element_type=jnp.float32
    )
    near_dprob = jnp.einsum(
        "bie,bje->bij", grad_heads, value_rows, preferred_element_type=jnp.float32
    )
    far_dprob = jnp.einsum("bie,ce->bic", grad_heads, value_sum, preferred_element_type=jnp.float32)
    correction = jnp.sum(near_prob * near_dprob, axis=-1) + jnp.sum(far_prob * far_dprob, axis=-1)
    near_grad = (near_prob * (near_dprob - correction[..., None])).astype(jnp.bfloat16)
    far_grad = (far_prob * (far_dprob - correction[..., None])).astype(jnp.bfloat16)
    grad_query = jnp.einsum("bij,bje->bie", near_grad, key_rows, preferred_element_type=jnp.float32)
    grad_query = (
        grad_query
        + jnp.einsum("bic,ce->bie", far_grad, key_sum, preferred_element_type=jnp.float32)
    ) * scaling
    grad_key = (
        jnp.einsum("bij,bie->bje", near_grad, queries, preferred_element_type=jnp.float32) * scaling
    )
    grad_ksum = (
        jnp.einsum("bic,bie->ce", far_grad, queries, preferred_element_type=jnp.float32) * scaling
    )
    return (grad_query.astype(jnp.bfloat16), grad_key, grad_value, grad_ksum, grad_vsum)


def shards(
    tokens, cotangent, span_ids, gain_one, w_qkv, w_out, b_out, gain_two, w_up, b_up, w_down, b_down
):
    incoming = tokens[0].astype(jnp.float32)
    row_count = incoming.shape[0]
    full_qkv, full_out, full_up, full_down = (
        lax.all_gather(w_qkv, "dp", axis=0, tiled=True),
        lax.all_gather(w_out, "dp", axis=1, tiled=True),
        lax.all_gather(w_up, "dp", axis=0, tiled=True),
        lax.all_gather(w_down, "dp", axis=1, tiled=True),
    )
    unit_one, inverse_one, normed = normalize(incoming, gain_one)
    normed_low = normed.astype(jnp.bfloat16)
    span_all = span_ids[0]
    member_all = (span_all[:, :, None] == jnp.arange(SPB, dtype=jnp.int32)[None, None, :]).astype(
        jnp.float32
    )
    counts_all = jnp.sum(member_all, axis=1)
    total_blocks = span_all.shape[0]
    qkv_whole, out_whole, up_whole, down_whole, bias_whole = (
        full_qkv,
        full_out,
        full_up,
        full_down,
        b_up,
    )
    rows_one = pair_rows(normed_low)
    width = qkv_whole.shape[0]
    qkv_flat = qkv_whole.reshape(width, -1)
    length = rows_one.shape[0]
    blocks = length // BLK
    heads_here = qkv_whole.shape[2] // HD
    projected = jnp.dot(rows_one, qkv_flat, preferred_element_type=jnp.float32).astype(jnp.bfloat16)
    per_head = jnp.moveaxis(projected.reshape(blocks, BLK, 3, heads_here, HD), (2, 3), (0, 1))
    member_low = member_all.astype(jnp.bfloat16)
    allowed = jnp.arange(blocks)[:, None] > (jnp.arange(total_blocks * SPB) // SPB)[None, :]
    key_sums, value_sums = lax.map(
        lambda pieces: span_means(pieces[0], pieces[1], member_low, counts_all),
        (per_head[1], per_head[2]),
    )

    def forward_head(pieces):
        return attend(pieces[0], pieces[1], pieces[2], pieces[3], pieces[4], counts_all, allowed)

    attended, log_total = lax.map(
        forward_head, (per_head[0], per_head[1], per_head[2], key_sums, value_sums)
    )
    attended_flat = jnp.moveaxis(attended, 0, 2).reshape(length, -1)

    def project_attn(offset, amount):
        return jnp.dot(attended_flat, out_whole, preferred_element_type=jnp.float32)

    attn_total = pair_sums(project_attn, row_count)
    middle = incoming + (attn_total + b_out)
    unit_two, inverse_two, normed_two = normalize(middle, gain_two)
    rows_two = pair_rows(normed_two.astype(jnp.bfloat16))
    before_gelu = jnp.dot(rows_two, up_whole, preferred_element_type=jnp.float32) + bias_whole
    activated, gelu_pull = jax.vjp(jax.nn.gelu, before_gelu)
    hidden = activated.astype(jnp.bfloat16)

    def project_mlp(offset, amount):
        return jnp.dot(hidden, down_whole, preferred_element_type=jnp.float32)

    mlp_total = pair_sums(project_mlp, row_count)
    output = middle + (mlp_total + b_down)
    grad_rows = cotangent[0]
    grad_output = grad_rows.astype(jnp.float32)
    full_grad = pair_rows(grad_rows)
    grad_down = jnp.einsum("sf,sd->fd", hidden, full_grad, preferred_element_type=jnp.float32)
    grad_hidden = jnp.einsum("sd,fd->sf", full_grad, down_whole, preferred_element_type=jnp.float32)
    grad_inner = gelu_pull(grad_hidden)[0].astype(jnp.bfloat16)
    bias_up = jnp.sum(grad_inner, axis=0, dtype=jnp.float32)
    grad_up = jnp.einsum("sd,sf->df", rows_two, grad_inner, preferred_element_type=jnp.float32)

    def back_mlp_rows(offset, amount):
        return jnp.einsum("sf,df->sd", grad_inner, up_whole, preferred_element_type=jnp.float32)

    grad_second = pair_sums(back_mlp_rows, row_count)
    grad_norm_two, gain_two_part = normalize_back(grad_second, unit_two, inverse_two, gain_two)
    grad_mid = grad_output + grad_norm_two
    grad_branch = grad_mid.astype(jnp.bfloat16)
    full_branch = pair_rows(grad_branch)
    grad_wout = jnp.einsum(
        "sh,sd->hd", attended_flat, full_branch, preferred_element_type=jnp.float32
    )
    grad_attended = jnp.einsum(
        "sd,hd->sh", full_branch, out_whole, preferred_element_type=jnp.float32
    ).astype(jnp.bfloat16)
    grad_heads = jnp.moveaxis(grad_attended.reshape(blocks, BLK, heads_here, HD), 2, 0)

    def backward_head(pieces):
        return head_backward(
            pieces[0],
            pieces[1],
            pieces[2],
            pieces[3],
            pieces[4],
            pieces[5],
            pieces[6],
            counts_all,
            allowed,
        )

    grad_query, grad_key, grad_value, grad_ksums, grad_vsums = lax.map(
        backward_head,
        (per_head[0], per_head[1], per_head[2], grad_heads, log_total, key_sums, value_sums),
    )
    share_key = grad_ksums.reshape(heads_here, blocks, SPB, HD) / counts_all[None, :, :, None]
    share_value = grad_vsums.reshape(heads_here, blocks, SPB, HD) / counts_all[None, :, :, None]
    grad_key = (grad_key + jnp.einsum("bjm,hbme->hbje", member_all, share_key)).astype(jnp.bfloat16)
    grad_value = (grad_value + jnp.einsum("bjm,hbme->hbje", member_all, share_value)).astype(
        jnp.bfloat16
    )
    grad_projected = jnp.moveaxis(
        jnp.stack((grad_query, grad_key, grad_value), axis=0), (0, 1), (2, 3)
    ).reshape(length, -1)
    grad_qkv = jnp.einsum(
        "sd,sc->dc", rows_one, grad_projected, preferred_element_type=jnp.float32
    ).reshape(qkv_whole.shape)

    def back_attn_rows(offset, amount):
        return jnp.einsum("sc,dc->sd", grad_projected, qkv_flat, preferred_element_type=jnp.float32)

    grad_first = pair_sums(back_attn_rows, row_count)
    grad_norm_one, gain_one_part = normalize_back(grad_first, unit_one, inverse_one, gain_one)
    grad_input = grad_mid + grad_norm_one
    half_width = bias_up.shape[0]
    bias_up_full = lax.dynamic_update_slice(
        jnp.zeros((half_width * lax.axis_size("tensor"),), jnp.float32),
        bias_up,
        (lax.axis_index("tensor") * half_width,),
    )
    totals = lax.psum(
        (
            gain_one_part,
            gain_two_part,
            jnp.sum(grad_branch, axis=0, dtype=jnp.float32),
            jnp.sum(grad_output, axis=0),
            bias_up_full,
        ),
        ("dp", "tensor"),
    )
    grad_qkv, grad_wout, grad_up, grad_down = (
        lax.psum_scatter(grad_qkv, "dp", scatter_dimension=0, tiled=True),
        lax.psum_scatter(grad_wout, "dp", scatter_dimension=1, tiled=True),
        lax.psum_scatter(grad_up, "dp", scatter_dimension=0, tiled=True),
        lax.psum_scatter(grad_down, "dp", scatter_dimension=1, tiled=True),
    )
    factor = 1.0 / math.sqrt(lax.axis_size("dp") * lax.axis_size("tensor") * row_count)
    return (
        output.astype(jnp.bfloat16)[None],
        grad_input.astype(jnp.bfloat16)[None],
        totals[0] * factor,
        grad_qkv * factor,
        grad_wout * factor,
        totals[2] * factor,
        totals[1] * factor,
        grad_up * factor,
        totals[4] * factor,
        grad_down * factor,
        totals[3] * factor,
    )


def solution(mesh):
    in_specs = (
        P("dp", "tensor", None),
        P("dp", "tensor", None),
        P("dp", None, None),
        P(),
        P("dp", None, "tensor"),
        P("tensor", "dp"),
        P(),
        P(),
        P("dp", "tensor"),
        P("tensor"),
        P("tensor", "dp"),
        P(),
    )
    out_specs = (
        P("dp", "tensor", None),
        P("dp", "tensor", None),
        P(),
        P("dp", None, "tensor"),
        P("tensor", "dp"),
        P(),
        P(),
        P("dp", "tensor"),
        P(),
        P("tensor", "dp"),
        P(),
    )
    return jax.shard_map(shards, mesh=mesh, in_specs=in_specs, out_specs=out_specs, check_vma=False)
```

profile of v0, /device:TPU:0, one launch (start us, length us, event | category | flops | bytes accessed | tf_op | source)
XLA Modules:
  0.0 714.1 jit_solution(7615604891802510770)
XLA Ops:
  9.6 1.7 fusion.119
  13.1 47.0 %all_gather.25 = bf16[512,3,256]{2,0,1:T(8,128)(2,1)S(1)} all-gather(bf16[32,3,256]{2,0,1:T(8,128)(2,1)S(1)} %copy-done.14), channel_id=1, replica_groups=mesh['dp'=16,'tensor'=2] {'dp'}, dimensions={0}, use_global_device_ids=true | all-gather | bytes 835584 | tf_op jit(solution)/shard_map/all_gather | solution.py:127
  60.4 36.9 %all_gather.26 = bf16[256,512]{0,1:T(8,128)(2,1)S(1)} all-gather(bf16[256,32]{0,1:T(8,128)(2,1)S(1)} %copy-done.18), channel_id=1, replica_groups=mesh['dp'=16,'tensor'=2] {'dp'}, dimensions={1}, use_global_device_ids=true | all-gather | bytes 278528 | tf_op jit(solution)/shard_map/all_gather | solution.py:128
  97.3 5.1 convolution_convert_fusion
  102.4 4.7 copy.64
  107.1 3.0 copy.111
  115.9 14.6 %while.50 = (s32[]{:T(128)}, bf16[4,8,256,64]{2,3,1,0:T(8,128)(2,1)}, f32[4,8,256]{2,1,0:T(8,128)S(1)}, bf16[4,8,256,64]{2,3,1,0:T(8,128)(2,1)S(1)}, bf16[4,8,25...) while((s32[]{:T(128)}, ...), condition=%wide.region_10.11_spmd.clone, body=%wide.region_5.10_spmd.clone.sunk | while | flops 147880064 | bytes 9204541 | solution.py:165
  117.3 2.2 fusion.226
  120.9 2.2 fusion.226
  124.6 2.2 fusion.226
  128.2 2.2 fusion.226
  130.4 2.2 copy.70
  133.9 2.1 convolution_convert_fusion.3
  136.7 6.9 reduce-scatter.9.cloned.1.call-done
  143.7 1.7 fusion.141
  149.1 43.8 %all-gather.12.cloned.1.call-done = bf16[512,1024]{1,0:T(8,128)(2,1)} async-done(((bf16[32,1024]{1,0:T(8,128)(2,1)}), bf16[512,1024]{1,0:T(8,128)(2,1)}) %all-gather.12.cloned.1.call-update) | async-done | bytes 1048592 | tf_op jit(solution)/shard_map/all_gather | solution.py:129
  192.9 11.4 %all-gather.10.cloned.1.call-done = bf16[2048,512]{1,0:T(8,128)(2,1)} async-done(((bf16[1024,512]{1,0:T(8,128)(2,1)}), bf16[2048,512]{1,0:T(8,128)(2,1)}) %all-gather.10.cloned.1.call-update) | async-done | bytes 2097168 | tf_op jit(solution)/shard_map/all_gather | solution.py:33
  204.3 10.5 %multiply_convert_fusion.2 = (bf16[2048,1024]{1,0:T(8,128)(2,1)}, f32[2048,1024]{1,0:T(8,128)}) fusion(f32[1024]{0:T(1024)S(1)} %copy-done.22, bf16[2048,512]{1,0:T(8,128)(2,1)} %all-gather.10.cloned.1.call-done, bf16[512,1024]{1,0:T(8,128)(2,1)} %all-gather.12.cloned.1.call-done), kind=kOutput, calls=%fused_computation.129 | convolution fusion | flops 2168455168 | bytes 15732736 | tf_op jit(solution)/shard_map/dot_general | solution.py:177
  214.8 49.1 %all-gather.14.cloned.1.call-done = bf16[1024,512]{0,1:T(8,128)(2,1)} async-done(((bf16[1024,32]{0,1:T(8,128)(2,1)}), bf16[1024,512]{0,1:T(8,128)(2,1)}) %all-gather.14.cloned.1.call-update) | async-done | bytes 1048592 | tf_op jit(solution)/shard_map/all_gather | solution.py:130
  263.9 11.0 %all-gather.18.cloned.1.call-done = bf16[1,2048,512]{2,1,0:T(8,128)(2,1)} async-done(((bf16[1,1024,512]{2,1,0:T(8,128)(2,1)}), bf16[1,2048,512]{2,1,0:T(8,128)(2,1)}) %all-gather.18.cloned.1.call-update) | async-done | bytes 2097168 | tf_op jit(solution)/shard_map/all_gather | solution.py:33
  274.9 10.2 %convert_reduce_fusion = (f32[1024]{0:T(1024)S(1)}, bf16[2048,1024]{1,0:T(8,128)(2,1)S(1)}) fusion(f32[2048,1024]{1,0:T(8,128)} %get-tuple-element.582, f32[1024]{0:T(1024)S(1)} %copy-done.22, bf16[1024,512]{0,1:T(8,128)(2,1)} %all-gather.14.cloned.1.call-done, bf16[1,2048,512]{2,1,0:T(8,128)(2,1)} %all-gather.18.cloned.1.call-done), kind=kOutput, calls=%fused_computation.128 | convolution fusion | flops 2195717120 | bytes 15736832 | tf_op jit(solution)/shard_map/sd,fd->sf/dot_general | solution.py:190
  285.1 1.9 copy-done.25
  287.0 3.8 convolution_convert_fusion.1
  291.1 6.2 convolution_convert_fusion.2
  297.4 4.4 reduce-scatter.13.cloned.1.call-done
  301.8 2.9 fusion.124
  304.7 10.0 %reduce-scatter.11.cloned.1.call-done = bf16[1024,512]{1,0:T(8,128)(2,1)} async-done(((bf16[2048,512]{1,0:T(8,128)(2,1)}), bf16[1024,512]{1,0:T(8,128)(2,1)}) %reduce-scatter.11.cloned.1.call-update) | async-done | bytes 1048592 | tf_op jit(solution)/shard_map/reduce_scatter | solution.py:37
  314.7 4.2 convert_reduce_fusion.3
  319.0 6.6 fusion.131
  325.7 7.2 %fusion.155 = f32[512,1024]{1,0:T(8,128)} fusion(bf16[2048,512]{1,0:T(8,128)(2,1)} %all-gather.10.cloned.1.call-done, bf16[2048,1024]{1,0:T(8,128)(2,1)} %copy-done.25), kind=kOutput, calls=%fused_computation.228 | convolution fusion | flops 2147483648 | bytes 8388608 | tf_op jit(solution)/shard_map/sd,sf->df/dot_general | solution.py:193
  333.2 3.3 convolution_convert_fusion.5
  336.5 2.4 copy.71
  338.9 2.5 copy.113
  341.4 32.6 %while.51 = (s32[]{:T(128)}, bf16[4,8,256,64]{2,3,0,1:T(8,128)(2,1)}, f32[4,8,256,64]{2,3,0,1:T(8,128)}, f32[4,8,256,64]{2,3,0,1:T(8,128)}, f32[4,16,64]{2,1,0:T...) while((s32[]{:T(128)}, ...), condition=%wide.region_21.22_spmd.clone, body=%wide.region_18.21_spmd.clone.sunk | while | flops 361561216 | bytes 22604664 | solution.py:224
  374.0 3.6 fusion.154
  377.7 2.2 fusion.138
  380.0 2.3 fusion.137
  382.7 2.0 copy.81
  387.5 3.0 fusion.127
  390.9 5.0 convolution_convert_fusion.4
  397.7 17.2 %reduce-scatter.23.cloned.1.call-done = f32[1024,32]{0,1:T(8,128)} async-done(((f32[1024,512]{0,1:T(8,128)}), f32[1024,32]{0,1:T(8,128)}) %reduce-scatter.23.cloned.1.call-update) | async-done | bytes 131088 | tf_op jit(solution)/shard_map/reduce_scatter | solution.py:267
  416.5 78.2 %reduce-scatter.21.cloned.1.call-done = f32[32,1024]{1,0:T(8,128)} async-done(((f32[512,1024]{1,0:T(8,128)}), f32[32,1024]{1,0:T(8,128)}) %reduce-scatter.21.cloned.1.call-update) | async-done | bytes 131088 | tf_op jit(solution)/shard_map/reduce_scatter | solution.py:266
  496.2 74.7 %reduce-scatter.19.cloned.1.call-done = f32[256,32]{0,1:T(8,128)} async-done(((f32[256,512]{0,1:T(8,128)}), f32[256,32]{0,1:T(8,128)}) %reduce-scatter.19.cloned.1.call-update) | async-done | bytes 32784 | tf_op jit(solution)/shard_map/reduce_scatter | solution.py:265
  572.3 76.1 %reduce-scatter.17.cloned.1.call-done = f32[32,3,256]{2,0,1:T(8,128)} async-done(((f32[512,3,256]{2,0,1:T(8,128)}), f32[32,3,256]{2,0,1:T(8,128)}) %reduce-scatter.17.cloned.1.call-update) | async-done | bytes 98320 | tf_op jit(solution)/shard_map/reduce_scatter | solution.py:264
  650.0 7.2 %reduce-scatter.15.cloned.1.call-done = bf16[1024,512]{1,0:T(8,128)(2,1)} async-done(((bf16[2048,512]{1,0:T(8,128)(2,1)}), bf16[1024,512]{1,0:T(8,128)(2,1)}) %reduce-scatter.15.cloned.1.call-update) | async-done | bytes 1048592 | tf_op jit(solution)/shard_map/reduce_scatter | solution.py:37
  657.2 2.7 fusion.126
  659.8 40.7 %all-reduce = (f32[512]{0:T(512)S(1)}, f32[512]{0:T(512)S(1)}, f32[512]{0:T(512)S(1)}, f32[2048]{0:T(1024)S(1)}, f32[512]{0:T(512)S(1)}) all-reduce(f32[512]{0:T(512)S(1)} %get-tuple-element.489, f32[512]{0:T(512)S(1)} %get-tuple-element.564, f32[512]{0:T(512)S(1)} %get-tuple-element.487, ...), channel_id=1, replica_groups=mesh['dp'=16,'tensor'=2] {'dp','tensor'}, use_global_device_ids=true, to_apply=%region_26.27 | all-reduce | flops 4096 | bytes 32768 | tf_op jit(solution)/shard_map/psum | solution.py:253
  703.5 2.9 fusion.140
  (234 shorter events, 69.2 us)
Async XLA Ops:
  8.0 3.3 copy-start
  8.0 3.3 copy-start.16
  8.0 89.3 %all-gather.8.cloned.1.call-start = ((), (), s32[]{:S(2)}) async-start(), calls=%async_computation.8 | async-start | bytes 3145728 | tf_op jit(solution)/shard_map/all_gather | solution.py:33
  9.6 3.3 copy-start.12
  9.6 3.4 copy-start.14
  12.8 47.6 %copy-start.18 = (bf16[256,32]{0,1:T(8,128)(2,1)S(1)}, bf16[256,32]{0,1:T(8,128)(2,1)}, u32[]{:S(2)}) copy-start(bf16[256,32]{0,1:T(8,128)(2,1)} %param.23) | copy-start | bytes 49156
  12.8 130.9 %reduce-scatter.9.cloned.1.call-start = ((), (), s32[]{:S(2)}) async-start(), calls=%async_computation.9 | async-start | bytes 3145728 | tf_op jit(solution)/shard_map/reduce_scatter | solution.py:37
  60.4 42.1 %copy-start.10 = (bf16[512,3,256]{0,2,1:T(8,128)(2,1)}, bf16[512,3,256]{0,2,1:T(8,128)(2,1)S(1)}, u32[]{:S(2)}) copy-start(bf16[512,3,256]{0,2,1:T(8,128)(2,1)S(1)} %copy.63) | copy-start | bytes 2359300
  113.4 1.0 copy-start.5
  130.4 2.5 copy-start.2
  130.4 2.5 copy-start.23
  133.0 1.0 copy-start.7
  133.9 9.7 %copy-start.13 = (f32[512]{0:T(512)S(1)}, f32[512]{0:T(512)}, u32[]{:S(2)}) copy-start(f32[512]{0:T(512)} %param.24) | copy-start | bytes 6148
  136.1 56.8 %all-gather.12.cloned.1.call-start = ((), (), s32[]{:S(2)}) async-start(), calls=%async_computation.11 | async-start | bytes 1114112 | tf_op jit(solution)/shard_map/all_gather | solution.py:129
  136.7 9.4 %copy-start.17 = (f32[512]{0:T(512)S(1)}, f32[512]{0:T(512)}, u32[]{:S(2)}) copy-start(f32[512]{0:T(512)} %param.25) | copy-start | bytes 6148
  136.7 67.6 %all-gather.10.cloned.1.call-start = ((), (), s32[]{:S(2)}) async-start(), calls=%async_computation.10 | async-start | bytes 3145728 | tf_op jit(solution)/shard_map/all_gather | solution.py:33
  143.7 1.7 copy-start.1
  146.1 58.2 %copy-start.22 = (f32[1024]{0:T(1024)S(1)}, f32[1024]{0:T(1024)}, u32[]{:S(2)}) copy-start(f32[1024]{0:T(1024)} %param.27) | copy-start | bytes 12292
  147.6 116.3 %all-gather.14.cloned.1.call-start = ((), (), s32[]{:S(2)}) async-start(), calls=%async_computation.12 | async-start | bytes 1114112 | tf_op jit(solution)/shard_map/all_gather | solution.py:130
  148.2 126.7 %all-gather.18.cloned.1.call-start = ((), (), s32[]{:S(2)}) async-start(), calls=%async_computation.21 | async-start | bytes 3145728 | tf_op jit(solution)/shard_map/all_gather | solution.py:33
  148.9 152.9 %reduce-scatter.13.cloned.1.call-start = ((), (), s32[]{:S(2)}) async-start(), calls=%async_computation.14 | async-start | bytes 3145728 | tf_op jit(solution)/shard_map/reduce_scatter | solution.py:37
  274.9 12.1 %copy-start.21 = (bf16[512,1024]{1,0:T(8,128)(2,1)S(1)}, bf16[512,1024]{1,0:T(8,128)(2,1)}, u32[]{:S(2)}) copy-start(bf16[512,1024]{1,0:T(8,128)(2,1)} %all-gather.12.cloned.1.call-done) | copy-start | bytes 3145732
  285.1 1.9 copy-start.25
  290.9 23.9 %reduce-scatter.11.cloned.1.call-start = ((), (), s32[]{:S(2)}) async-start(), calls=%async_computation.13 | async-start | bytes 3145728 | tf_op jit(solution)/shard_map/reduce_scatter | solution.py:37
  297.3 17.4 %copy-start.19 = (f32[512]{0:T(512)S(1)}, f32[512]{0:T(512)}, u32[]{:S(2)}) copy-start(f32[512]{0:T(512)} %param.29) | copy-start | bytes 6148
  297.4 35.9 %all-gather.16.cloned.1.call-start = ((), (), s32[]{:S(2)}) async-start(), calls=%async_computation.15 | async-start | bytes 3145728 | tf_op jit(solution)/shard_map/all_gather | solution.py:33
  318.9 95.9 %reduce-scatter.23.cloned.1.call-start = ((), (), s32[]{:S(2)}) async-start(), calls=%async_computation.20 | async-start | bytes 2228224 | tf_op jit(solution)/shard_map/reduce_scatter | solution.py:267
  325.6 169.1 %reduce-scatter.21.cloned.1.call-start = ((), (), s32[]{:S(2)}) async-start(), calls=%async_computation.19 | async-start | bytes 2228224 | tf_op jit(solution)/shard_map/reduce_scatter | solution.py:266
  332.9 238.1 %reduce-scatter.19.cloned.1.call-start = ((), (), s32[]{:S(2)}) async-start(), calls=%async_computation.18 | async-start | bytes 557056 | tf_op jit(solution)/shard_map/reduce_scatter | solution.py:265
  336.5 4.9 copy-start.3
  336.5 4.9 copy-start.15
  336.5 4.9 copy-start.24
  377.7 270.8 %reduce-scatter.17.cloned.1.call-start = ((), (), s32[]{:S(2)}) async-start(), calls=%async_computation.17 | async-start | bytes 1671168 | tf_op jit(solution)/shard_map/reduce_scatter | solution.py:264
  380.0 2.4 copy-start.9
  384.7 2.8 copy-start.20
  385.8 1.7 copy-start.8
  387.5 3.4 copy-start.11
  390.6 266.6 %reduce-scatter.15.cloned.1.call-start = ((), (), s32[]{:S(2)}) async-start(), calls=%async_computation.16 | async-start | bytes 3145728 | tf_op jit(solution)/shard_map/reduce_scatter | solution.py:37
  395.9 1.2 copy-start.4
  657.2 46.3 %copy-start.6 = (bf16[1024,512]{1,0:T(8,128)(2,1)S(1)}, bf16[1024,512]{1,0:T(8,128)(2,1)}, u32[]{:S(2)}) copy-start(bf16[1024,512]{1,0:T(8,128)(2,1)} %reduce-scatter.15.cloned.1.call-done) | copy-start | bytes 3145732
Sparse Core Ops, SparseCore 0:
  12.9 13.2 all-gather.7
  136.2 7.4 reduce-scatter.8
  291.0 10.8 reduce-scatter.12
  303.9 10.7 reduce-scatter.10
Sparse Core Ops, SparseCore 1:
  139.7 53.1 all-gather.11
  195.0 9.3 all-gather.9
  207.3 56.5 all-gather.13
  265.6 9.3 all-gather.17
  319.0 11.6 all-gather.15
  333.1 81.7 reduce-scatter.22
  417.1 77.5 reduce-scatter.20
  497.4 73.5 reduce-scatter.18
  573.1 75.3 reduce-scatter.16
  650.8 6.3 reduce-scatter.14
where the time goes:
time: 723 us; the launch traced here: 714 us
  waiting for transfers between devices  392 us (54%)
  blocking collectives  125 us (17%)
  matrix products  112 us (15%)
  other arithmetic  34.3 us (5%)
  local copies, waits for them, and re-layouts  32.8 us (5%)
  between operations  16.3 us (2%)
    reduce_scatter x1, waiting for transfers between devices, shards(): lax.psum_scatter(grad_up, 'dp', scatter_dimension=0, tiled=True)  78.2 us
    reduce_scatter x1, waiting for transfers between devices, shards(): lax.psum_scatter(grad_qkv, 'dp', scatter_dimension=0, tiled=True)  76.1 us
    reduce_scatter x1, waiting for transfers between devices, shards(): lax.psum_scatter(grad_wout, 'dp', scatter_dimension=1, tiled=True)  74.7 us
    all_gather x1, waiting for transfers between devices, shards(): lax.all_gather(w_down, 'dp', axis=1, tiled=True)  49.1 us
    all_gather x1, blocking collectives, shards(): lax.all_gather(w_qkv, 'dp', axis=0, tiled=True)  47 us
    all_gather x1, waiting for transfers between devices, shards(): lax.all_gather(w_up, 'dp', axis=0, tiled=True)  43.8 us
    psum x1, blocking collectives, shards(): lax.psum((gain_one_part, gain_two_part, jnp.sum(grad_branch, axis=0, dtyp...  40.7 us
    all_gather x1, blocking collectives, shards(): lax.all_gather(w_out, 'dp', axis=1, tiled=True)  36.9 us
  transfers between devices with their start and end apart: 14, of which 12 were waited for; matrix products, arithmetic and copies ran while one was open for 15% of the time, Pallas kernels for 0%

commit v1 on v0

--- a/solution.py
+++ b/solution.py
@@ -251,14 +251,17 @@
         (lax.axis_index("tensor") * half_width,),
     )
     totals = lax.psum(
-        (
-            gain_one_part,
-            gain_two_part,
-            jnp.sum(grad_branch, axis=0, dtype=jnp.float32),
-            jnp.sum(grad_output, axis=0),
-            bias_up_full,
+        lax.psum(
+            (
+                gain_one_part,
+                gain_two_part,
+                jnp.sum(grad_branch, axis=0, dtype=jnp.float32),
+                jnp.sum(grad_output, axis=0),
+                bias_up_full,
+            ),
+            "tensor",
         ),
-        ("dp", "tensor"),
+        "dp",
     )
     grad_qkv, grad_wout, grad_up, grad_down = (
         lax.psum_scatter(grad_qkv, "dp", scatter_dimension=0, tiled=True),

time: 723 us -> 763 us (1.055)
  blocking collectives: 125 us -> 164 us
    psum x0 -> x1, blocking collectives: none -> 77.1 us  [shards(): lax.psum(lax.psum((gain_one_part, gain_two_part, jnp.sum(grad_branch, axi...]
    psum x1, blocking collectives: 40.7 us -> 3.37 us  [shards(): lax.psum((gain_one_part, gain_two_part, jnp.sum(grad_branch, axis=0, dtyp...]
  transfers between devices with their start and end apart: 14 -> 14, of which waited for: 12 -> 12; matrix products, arithmetic and copies ran while one was open for 15% -> 14% of each run, Pallas kernels for 0% -> 0%
where the time goes in v1:
time: 763 us; the launch traced here: 754 us
  waiting for transfers between devices  392 us (51%)
  blocking collectives  164 us (21%)
  matrix products  112 us (15%)
  other arithmetic  34.3 us (4%)
  local copies, waits for them, and re-layouts  32.8 us (4%)
  between operations  16.3 us (2%)
    reduce_scatter x1, waiting for transfers between devices, shards(): lax.psum_scatter(grad_up, 'dp', scatter_dimension=0, tiled=True)  78.2 us
    psum x1, blocking collectives, shards(): lax.psum(lax.psum((gain_one_part, gain_two_part, jnp.sum(grad_branch, axi...  77.1 us
    reduce_scatter x1, waiting for transfers between devices, shards(): lax.psum_scatter(grad_qkv, 'dp', scatter_dimension=0, tiled=True)  76.1 us
    reduce_scatter x1, waiting for transfers between devices, shards(): lax.psum_scatter(grad_wout, 'dp', scatter_dimension=1, tiled=True)  74.7 us
    all_gather x1, waiting for transfers between devices, shards(): lax.all_gather(w_down, 'dp', axis=1, tiled=True)  49.1 us
    all_gather x1, blocking collectives, shards(): lax.all_gather(w_qkv, 'dp', axis=0, tiled=True)  47 us
    all_gather x1, waiting for transfers between devices, shards(): lax.all_gather(w_up, 'dp', axis=0, tiled=True)  43.8 us
    all_gather x1, blocking collectives, shards(): lax.all_gather(w_out, 'dp', axis=1, tiled=True)  36.9 us
  transfers between devices with their start and end apart: 14, of which 12 were waited for; matrix products, arithmetic and copies ran while one was open for 14% of the time, Pallas kernels for 0%

profile of v1, /device:TPU:0, one launch (start us, length us, event | category | flops | bytes accessed | tf_op | source)
XLA Modules:
  0.0 753.8 jit_solution(16592284424386134208)
XLA Ops:
  13.1 47.0 %all_gather.25 = bf16[512,3,256]{2,0,1:T(8,128)(2,1)S(1)} all-gather(bf16[32,3,256]{2,0,1:T(8,128)(2,1)S(1)} %copy-done.14), channel_id=1, replica_groups=mesh['dp'=16,'tensor'=2] {'dp'}, dimensions={0}, use_global_device_ids=true | all-gather | bytes 835584 | tf_op jit(solution)/shard_map/all_gather | solution.py:127
  60.4 36.9 %all_gather.26 = bf16[256,512]{0,1:T(8,128)(2,1)S(1)} all-gather(bf16[256,32]{0,1:T(8,128)(2,1)S(1)} %copy-done.18), channel_id=1, replica_groups=mesh['dp'=16,'tensor'=2] {'dp'}, dimensions={1}, use_global_device_ids=true | all-gather | bytes 278528 | tf_op jit(solution)/shard_map/all_gather | solution.py:128
  97.3 5.1 convolution_convert_fusion
  102.4 4.7 copy.64
  107.1 3.0 copy.111
  115.9 14.6 %while.50 = (s32[]{:T(128)}, bf16[4,8,256,64]{2,3,1,0:T(8,128)(2,1)}, f32[4,8,256]{2,1,0:T(8,128)S(1)}, bf16[4,8,256,64]{2,3,1,0:T(8,128)(2,1)S(1)}, bf16[4,8,25...) while((s32[]{:T(128)}, ...), condition=%wide.region_10.11_spmd.clone, body=%wide.region_5.10_spmd.clone.sunk | while | flops 147880064 | bytes 9204541 | solution.py:165
  117.3 2.2 fusion.226
  120.9 2.2 fusion.226
  124.6 2.2 fusion.226
  128.2 2.2 fusion.226
  130.4 2.2 copy.70
  133.9 2.1 convolution_convert_fusion.3
  136.7 6.9 reduce-scatter.9.cloned.1.call-done
  143.7 1.7 fusion.141
  149.1 43.8 %all-gather.12.cloned.1.call-done = bf16[512,1024]{1,0:T(8,128)(2,1)} async-done(((bf16[32,1024]{1,0:T(8,128)(2,1)}), bf16[512,1024]{1,0:T(8,128)(2,1)}) %all-gather.12.cloned.1.call-update) | async-done | bytes 1048592 | tf_op jit(solution)/shard_map/all_gather | solution.py:129
  192.9 11.4 %all-gather.10.cloned.1.call-done = bf16[2048,512]{1,0:T(8,128)(2,1)} async-done(((bf16[1024,512]{1,0:T(8,128)(2,1)}), bf16[2048,512]{1,0:T(8,128)(2,1)}) %all-gather.10.cloned.1.call-update) | async-done | bytes 2097168 | tf_op jit(solution)/shard_map/all_gather | solution.py:33
  204.3 10.5 %multiply_convert_fusion.2 = (bf16[2048,1024]{1,0:T(8,128)(2,1)}, f32[2048,1024]{1,0:T(8,128)}) fusion(f32[1024]{0:T(1024)S(1)} %copy-done.22, bf16[2048,512]{1,0:T(8,128)(2,1)} %all-gather.10.cloned.1.call-done, bf16[512,1024]{1,0:T(8,128)(2,1)} %all-gather.12.cloned.1.call-done), kind=kOutput, calls=%fused_computation.129 | convolution fusion | flops 2168455168 | bytes 15732736 | tf_op jit(solution)/shard_map/dot_general | solution.py:177
  214.8 49.1 %all-gather.14.cloned.1.call-done = bf16[1024,512]{0,1:T(8,128)(2,1)} async-done(((bf16[1024,32]{0,1:T(8,128)(2,1)}), bf16[1024,512]{0,1:T(8,128)(2,1)}) %all-gather.14.cloned.1.call-update) | async-done | bytes 1048592 | tf_op jit(solution)/shard_map/all_gather | solution.py:130
  263.9 11.0 %all-gather.18.cloned.1.call-done = bf16[1,2048,512]{2,1,0:T(8,128)(2,1)} async-done(((bf16[1,1024,512]{2,1,0:T(8,128)(2,1)}), bf16[1,2048,512]{2,1,0:T(8,128)(2,1)}) %all-gather.18.cloned.1.call-update) | async-done | bytes 2097168 | tf_op jit(solution)/shard_map/all_gather | solution.py:33
  274.9 10.2 %convert_reduce_fusion = (f32[1024]{0:T(1024)S(1)}, bf16[2048,1024]{1,0:T(8,128)(2,1)S(1)}) fusion(f32[2048,1024]{1,0:T(8,128)} %get-tuple-element.587, f32[1024]{0:T(1024)S(1)} %copy-done.22, bf16[1024,512]{0,1:T(8,128)(2,1)} %all-gather.14.cloned.1.call-done, bf16[1,2048,512]{2,1,0:T(8,128)(2,1)} %all-gather.18.cloned.1.call-done), kind=kOutput, calls=%fused_computation.128 | convolution fusion | flops 2195717120 | bytes 15736832 | tf_op jit(solution)/shard_map/sd,fd->sf/dot_general | solution.py:190
  285.1 1.9 copy-done.25
  287.0 3.8 convolution_convert_fusion.1
  291.1 6.2 convolution_convert_fusion.2
  297.4 4.4 reduce-scatter.13.cloned.1.call-done
  301.8 2.9 fusion.124
  304.7 10.0 %reduce-scatter.11.cloned.1.call-done = bf16[1024,512]{1,0:T(8,128)(2,1)} async-done(((bf16[2048,512]{1,0:T(8,128)(2,1)}), bf16[1024,512]{1,0:T(8,128)(2,1)}) %reduce-scatter.11.cloned.1.call-update) | async-done | bytes 1048592 | tf_op jit(solution)/shard_map/reduce_scatter | solution.py:37
  314.7 4.2 convert_reduce_fusion.3
  319.0 6.6 fusion.131
  325.7 7.2 fusion.155
  333.2 3.3 convolution_convert_fusion.5
  336.5 2.4 copy.71
  338.9 2.5 copy.113
  341.4 32.6 %while.51 = (s32[]{:T(128)}, bf16[4,8,256,64]{2,3,0,1:T(8,128)(2,1)}, f32[4,8,256,64]{2,3,0,1:T(8,128)}, f32[4,8,256,64]{2,3,0,1:T(8,128)}, f32[4,16,64]{2,1,0:T...) while((s32[]{:T(128)}, ...), condition=%wide.region_21.22_spmd.clone, body=%wide.region_18.21_spmd.clone.sunk | while | flops 361561216 | bytes 22604664 | solution.py:224
  374.0 3.6 fusion.154
  377.7 2.2 fusion.138
  380.0 2.3 fusion.137
  382.7 2.0 copy.81
  387.5 3.0 fusion.127
  390.9 5.0 convolution_convert_fusion.4
  397.7 17.2 %reduce-scatter.23.cloned.1.call-done = f32[1024,32]{0,1:T(8,128)} async-done(((f32[1024,512]{0,1:T(8,128)}), f32[1024,32]{0,1:T(8,128)}) %reduce-scatter.23.cloned.1.call-update) | async-done | bytes 131088 | tf_op jit(solution)/shard_map/reduce_scatter | solution.py:270
  416.5 78.2 %reduce-scatter.21.cloned.1.call-done = f32[32,1024]{1,0:T(8,128)} async-done(((f32[512,1024]{1,0:T(8,128)}), f32[32,1024]{1,0:T(8,128)}) %reduce-scatter.21.cloned.1.call-update) | async-done | bytes 131088 | tf_op jit(solution)/shard_map/reduce_scatter | solution.py:269
  496.2 74.7 %reduce-scatter.19.cloned.1.call-done = f32[256,32]{0,1:T(8,128)} async-done(((f32[256,512]{0,1:T(8,128)}), f32[256,32]{0,1:T(8,128)}) %reduce-scatter.19.cloned.1.call-update) | async-done | bytes 32784 | tf_op jit(solution)/shard_map/reduce_scatter | solution.py:268
  572.3 76.1 %reduce-scatter.17.cloned.1.call-done = f32[32,3,256]{2,0,1:T(8,128)} async-done(((f32[512,3,256]{2,0,1:T(8,128)}), f32[32,3,256]{2,0,1:T(8,128)}) %reduce-scatter.17.cloned.1.call-update) | async-done | bytes 98320 | tf_op jit(solution)/shard_map/reduce_scatter | solution.py:267
  650.0 7.2 reduce-scatter.15.cloned.1.call-done
  657.2 2.7 fusion.126
  659.8 3.4 all-reduce.1
  663.2 77.1 %all-reduce = (f32[512]{0:T(512)S(1)}, f32[512]{0:T(512)S(1)}, f32[512]{0:T(512)S(1)}, f32[2048]{0:T(1024)S(1)}, f32[512]{0:T(512)S(1)}) all-reduce(f32[512]{0:T(512)S(1)} %get-tuple-element.562, f32[512]{0:T(512)S(1)} %get-tuple-element.563, f32[512]{0:T(512)S(1)} %get-tuple-element.564, ...), channel_id=1, replica_groups=mesh['dp'=16,'tensor'=2] {'dp'}, use_global_device_ids=true, to_apply=%region_27.28 | all-reduce | flops 4096 | bytes 32768 | tf_op jit(solution)/shard_map/psum | solution.py:253
  743.2 2.9 fusion.140
  (235 shorter events, 70.9 us)
Async XLA Ops:
  8.0 3.3 copy-start
  8.0 3.3 copy-start.16
  8.0 89.3 %all-gather.8.cloned.1.call-start = ((), (), s32[]{:S(2)}) async-start(), calls=%async_computation.8 | async-start | bytes 3145728 | tf_op jit(solution)/shard_map/all_gather | solution.py:33
  9.6 3.3 copy-start.12
  9.6 3.4 copy-start.14
  12.8 47.6 %copy-start.18 = (bf16[256,32]{0,1:T(8,128)(2,1)S(1)}, bf16[256,32]{0,1:T(8,128)(2,1)}, u32[]{:S(2)}) copy-start(bf16[256,32]{0,1:T(8,128)(2,1)} %param.23) | copy-start | bytes 49156
  12.8 130.9 %reduce-scatter.9.cloned.1.call-start = ((), (), s32[]{:S(2)}) async-start(), calls=%async_computation.9 | async-start | bytes 3145728 | tf_op jit(solution)/shard_map/reduce_scatter | solution.py:37
  60.4 42.1 %copy-start.10 = (bf16[512,3,256]{0,2,1:T(8,128)(2,1)}, bf16[512,3,256]{0,2,1:T(8,128)(2,1)S(1)}, u32[]{:S(2)}) copy-start(bf16[512,3,256]{0,2,1:T(8,128)(2,1)S(1)} %copy.63) | copy-start | bytes 2359300
  113.4 1.0 copy-start.5
  130.4 2.5 copy-start.2
  130.4 2.5 copy-start.23
  133.0 1.0 copy-start.7
  133.9 9.7 %copy-start.13 = (f32[512]{0:T(512)S(1)}, f32[512]{0:T(512)}, u32[]{:S(2)}) copy-start(f32[512]{0:T(512)} %param.24) | copy-start | bytes 6148
  136.1 56.8 %all-gather.12.cloned.1.call-start = ((), (), s32[]{:S(2)}) async-start(), calls=%async_computation.11 | async-start | bytes 1114112 | tf_op jit(solution)/shard_map/all_gather | solution.py:129
  136.7 9.4 %copy-start.17 = (f32[512]{0:T(512)S(1)}, f32[512]{0:T(512)}, u32[]{:S(2)}) copy-start(f32[512]{0:T(512)} %param.25) | copy-start | bytes 6148
  136.7 67.6 %all-gather.10.cloned.1.call-start = ((), (), s32[]{:S(2)}) async-start(), calls=%async_computation.10 | async-start | bytes 3145728 | tf_op jit(solution)/shard_map/all_gather | solution.py:33
  143.7 1.7 copy-start.1
  146.1 58.2 %copy-start.22 = (f32[1024]{0:T(1024)S(1)}, f32[1024]{0:T(1024)}, u32[]{:S(2)}) copy-start(f32[1024]{0:T(1024)} %param.27) | copy-start | bytes 12292
  147.6 116.3 %all-gather.14.cloned.1.call-start = ((), (), s32[]{:S(2)}) async-start(), calls=%async_computation.12 | async-start | bytes 1114112 | tf_op jit(solution)/shard_map/all_gather | solution.py:130
  148.2 126.7 %all-gather.18.cloned.1.call-start = ((), (), s32[]{:S(2)}) async-start(), calls=%async_computation.21 | async-start | bytes 3145728 | tf_op jit(solution)/shard_map/all_gather | solution.py:33
  148.9 152.9 %reduce-scatter.13.cloned.1.call-start = ((), (), s32[]{:S(2)}) async-start(), calls=%async_computation.14 | async-start | bytes 3145728 | tf_op jit(solution)/shard_map/reduce_scatter | solution.py:37
  274.9 12.1 %copy-start.21 = (bf16[512,1024]{1,0:T(8,128)(2,1)S(1)}, bf16[512,1024]{1,0:T(8,128)(2,1)}, u32[]{:S(2)}) copy-start(bf16[512,1024]{1,0:T(8,128)(2,1)} %all-gather.12.cloned.1.call-done) | copy-start | bytes 3145732
  285.1 1.9 copy-start.25
  290.9 23.9 %reduce-scatter.11.cloned.1.call-start = ((), (), s32[]{:S(2)}) async-start(), calls=%async_computation.13 | async-start | bytes 3145728 | tf_op jit(solution)/shard_map/reduce_scatter | solution.py:37
  297.3 17.4 %copy-start.19 = (f32[512]{0:T(512)S(1)}, f32[512]{0:T(512)}, u32[]{:S(2)}) copy-start(f32[512]{0:T(512)} %param.29) | copy-start | bytes 6148
  297.4 35.9 %all-gather.16.cloned.1.call-start = ((), (), s32[]{:S(2)}) async-start(), calls=%async_computation.15 | async-start | bytes 3145728 | tf_op jit(solution)/shard_map/all_gather | solution.py:33
  318.9 95.9 %reduce-scatter.23.cloned.1.call-start = ((), (), s32[]{:S(2)}) async-start(), calls=%async_computation.20 | async-start | bytes 2228224 | tf_op jit(solution)/shard_map/reduce_scatter | solution.py:270
  325.6 169.1 %reduce-scatter.21.cloned.1.call-start = ((), (), s32[]{:S(2)}) async-start(), calls=%async_computation.19 | async-start | bytes 2228224 | tf_op jit(solution)/shard_map/reduce_scatter | solution.py:269
  332.9 238.1 %reduce-scatter.19.cloned.1.call-start = ((), (), s32[]{:S(2)}) async-start(), calls=%async_computation.18 | async-start | bytes 557056 | tf_op jit(solution)/shard_map/reduce_scatter | solution.py:268
  336.5 4.9 copy-start.3
  336.5 4.9 copy-start.15
  336.5 4.9 copy-start.24
  377.7 270.8 %reduce-scatter.17.cloned.1.call-start = ((), (), s32[]{:S(2)}) async-start(), calls=%async_computation.17 | async-start | bytes 1671168 | tf_op jit(solution)/shard_map/reduce_scatter | solution.py:267
  380.0 2.4 copy-start.9
  384.7 2.8 copy-start.20
  385.8 1.7 copy-start.8
  387.5 3.4 copy-start.11
  390.6 266.6 %reduce-scatter.15.cloned.1.call-start = ((), (), s32[]{:S(2)}) async-start(), calls=%async_computation.16 | async-start | bytes 3145728 | tf_op jit(solution)/shard_map/reduce_scatter | solution.py:37
  395.9 1.2 copy-start.4
  657.2 86.0 %copy-start.6 = (bf16[1024,512]{1,0:T(8,128)(2,1)S(1)}, bf16[1024,512]{1,0:T(8,128)(2,1)}, u32[]{:S(2)}) copy-start(bf16[1024,512]{1,0:T(8,128)(2,1)} %reduce-scatter.15.cloned.1.call-done) | copy-start | bytes 3145732
Sparse Core Ops, SparseCore 0:
  12.9 13.2 all-gather.7
  136.2 7.4 reduce-scatter.8
  291.0 10.8 reduce-scatter.12
  303.9 10.7 reduce-scatter.10
Sparse Core Ops, SparseCore 1:
  139.7 53.1 all-gather.11
  195.0 9.3 all-gather.9
  207.3 56.5 all-gather.13
  265.6 9.3 all-gather.17
  319.0 11.6 all-gather.15
  333.1 81.7 reduce-scatter.22
  417.1 77.5 reduce-scatter.20
  497.4 73.5 reduce-scatter.18
  573.1 75.3 reduce-scatter.16
  650.8 6.3 reduce-scatter.14
